TPU v7x, 512 devices: a whole 4x8x8 slice. The times are simulated.
512 devices in a mesh: occ: 8 (over z), vir: 64 (over y, x, core).
Axes of the slice: x: 4, y: 8, z: 8, core: 2. Of those that a mesh axis runs over, the one named last changes fastest.
Arguments:
- amplitudes: bfloat16 [6144, 2048], P('occ', 'vir'), may hold values from -6 to 6
- integrals: bfloat16 [2048, 163840], P('occ', 'vir'), may hold values from -0.375 to 0.375
- occ_sym: int32 [48], P('occ'), may hold values from 0 to 7, as said below
- vir_sym: int32 [1280], P('vir'), may hold values from 0 to 7, as said below
- k_sym: int32 [16], replicated, may hold values from 0 to 7
Outputs:
- ladder: bfloat16 [6144, 163840], P('occ', 'vir')
Inputs may be any that keep to these rules, and one draw needn't show every extreme that they name: `occ_sym`: among the 6 blocks of one index of occ no irrep occurs more than 2 times, and one occurs exactly 2 times. `vir_sym`: among the 20 blocks of one index of vir no irrep occurs more than 5 times, and one occurs exactly 5 times.
All inputs are finite; a program needn't handle non-finite values.
Results may differ from a plain program's by a relative error of at most 0.001.
Values may be sent and summed in bfloat16 or wider, within the bound.
A program may use at most 64 MiB of HBM per device.

v0:
```python
import jax
import jax.numpy as jnp
from jax import lax
from jax.sharding import PartitionSpec as P

BLK = 128
MAXB = 5


def slot_order(symmetry, labels, slot_bound):
    label_count = labels.shape[0]
    positions = jnp.arange(label_count, dtype=jnp.int32)
    matching = labels == symmetry
    ranking = jnp.where(matching, positions, positions + label_count)
    chosen = jnp.argsort(ranking)[:slot_bound]
    return (chosen, matching[chosen])


def slot_table(symmetry, labels, slot_bound):
    chosen, usable = slot_order(symmetry, labels, slot_bound)
    positions = jnp.arange(labels.shape[0], dtype=jnp.int32)
    return ((chosen[:, None] == positions[None, :]) & usable[:, None]).astype(jnp.bfloat16)


def per_device(amplitudes, integrals, occ_sym, vir_sym, k_sym):
    occ_rows = amplitudes.shape[0]
    occ_blocks = occ_rows // BLK
    kblocks = k_sym.shape[0]
    window = kblocks * BLK
    vir_blocks = vir_sym.shape[0]
    col_width = vir_blocks * BLK
    block_ids = jnp.arange(kblocks, dtype=jnp.int32)

    def column_table(symmetry):
        return slot_table(symmetry, vir_sym, MAXB)

    gathered = lax.all_gather(amplitudes, "vir", axis=1, tiled=True)
    allowed = (occ_sym[:, None] == k_sym[None, :]).astype(jnp.bfloat16)
    amp_masked = (
        gathered.reshape(occ_blocks, BLK, kblocks, BLK) * allowed[:, None, :, None]
    ).reshape(occ_rows, window)
    shard_rows = integrals.shape[0]
    own_count = shard_rows // BLK
    first_block = lax.axis_index("occ") * own_count
    own_ids = first_block + jnp.arange(own_count, dtype=jnp.int32)
    own_syms = jnp.sum(jnp.where(own_ids[:, None] == block_ids[None, :], k_sym[None, :], 0), axis=1)
    start_sum = jnp.zeros((occ_rows, vir_blocks, BLK), jnp.float32)
    tables_v = jax.vmap(column_table)(own_syms)
    packed_v = jnp.einsum(
        "bmv,brvc->brmc",
        tables_v,
        integrals.reshape(own_count, BLK, vir_blocks, BLK),
        preferred_element_type=jnp.float32,
    )
    packed_v = packed_v.astype(jnp.bfloat16).reshape(shard_rows, MAXB * BLK)
    shard_piece = lax.all_gather(packed_v, "occ", axis=0, tiled=True)
    piece_blocks = shard_piece.shape[0] // BLK

    def one_block(block_index, running_sum):
        row_start = block_index * BLK
        symmetry = jnp.sum(jnp.where(block_ids == row_start // BLK, k_sym, 0))
        chosen = slot_order(symmetry, vir_sym, MAXB)[0]
        amp_cols = lax.dynamic_slice_in_dim(amp_masked, row_start, BLK, 1)
        block_part = lax.dynamic_slice_in_dim(shard_piece, block_index * BLK, BLK, 0)
        product = jnp.dot(amp_cols, block_part, preferred_element_type=jnp.float32)
        return running_sum.at[:, chosen, :].add(product.reshape(occ_rows, MAXB, BLK))

    summed = lax.fori_loop(0, piece_blocks, one_block, start_sum)
    return summed.reshape(occ_rows, col_width).astype(jnp.bfloat16)


def solution(mesh):
    return jax.shard_map(
        per_device,
        mesh=mesh,
        in_specs=(P("occ", "vir"), P("occ", "vir"), P("occ"), P("vir"), P()),
        out_specs=P("occ", "vir"),
        check_vma=False,
    )
```

profile of v0, /device:TPU:4, one launch (start us, length us, event | category | flops | bytes accessed | tf_op | source)
XLA Modules:
  0.0 402.5 jit_solution(3272119504203592197)
XLA Ops:
  10.9 2.6 reshape.82
  15.0 82.5 %all-gather.3.cloned.1.call-done = bf16[768,2048]{0,1:T(8,128)(2,1)} async-done(((bf16[768,32]{0,1:T(8,128)(2,1)}), bf16[768,2048]{0,1:T(8,128)(2,1)}) %all-gather.3.cloned.1.call-update) | async-done | bytes 3145744 | tf_op jit(solution)/shard_map/all_gather | solution.py:37
  97.5 3.2 copy.43
  101.2 2.4 bitcast_multiply_fusion
  103.5 49.2 %all-gather.5.cloned.1.call-done = bf16[2048,640]{0,1:T(8,128)(2,1)} async-done(((bf16[256,640]{0,1:T(8,128)(2,1)}), bf16[2048,640]{0,1:T(8,128)(2,1)}) %all-gather.5.cloned.1.call-update) | async-done | bytes 2621456 | tf_op jit(solution)/shard_map/all_gather | solution.py:56
  152.7 3.9 broadcast_in_dim.62
  156.6 225.5 %while.16 = (s32[]{:T(128)}, f32[768,20,128]{2,0,1:T(8,128)}, s32[16]{0:T(128)S(1)}, s32[20]{0:T(128)S(1)}, bf16[768,2048]{1,0:T(8,128)(2,1)}, /*index=5*/bf16[2...) while((s32[]{:T(128)}, f32[768,20,128]{2,0,1:T(8,128)}, ...), condition=%wide.region_6.7_spmd.clone, body=%wide.region_2.6_spmd.clone.sunk | while | flops 126320880 | bytes 12158960 | solution.py:68
  159.7 2.7 fusion.23
  162.4 1.9 copy.63
  164.3 6.4 %scatter_fusion = f32[768,20,128]{2,0,1:T(8,128)} fusion(f32[768,20,128]{2,0,1:T(8,128)} %get-tuple-element.294, s32[5]{0:T(128)S(1)} %compare_select_fusion.8, f32[5,768,128]{2,1,0:T(8,128)S(1)} %bitcast.27), kind=kCustom, calls=%fused_computation.1.clone.clone.1 | custom fusion | flops 491520 | bytes 5898260 | tf_op jit(solution)/shard_map/while/body/eval_jaxpr/scatter-add | solution.py:66
  173.8 2.7 fusion.23
  176.4 1.9 copy.63
  178.3 6.4 %scatter_fusion = f32[768,20,128]{2,0,1:T(8,128)} fusion(f32[768,20,128]{2,0,1:T(8,128)} %get-tuple-element.294, s32[5]{0:T(128)S(1)} %compare_select_fusion.8, f32[5,768,128]{2,1,0:T(8,128)S(1)} %bitcast.27), kind=kCustom, calls=%fused_computation.1.clone.clone.1 | custom fusion | flops 491520 | bytes 5898260 | tf_op jit(solution)/shard_map/while/body/eval_jaxpr/scatter-add | solution.py:66
  187.8 2.7 fusion.23
  190.5 1.9 copy.63
  192.4 6.4 %scatter_fusion = f32[768,20,128]{2,0,1:T(8,128)} fusion(f32[768,20,128]{2,0,1:T(8,128)} %get-tuple-element.294, s32[5]{0:T(128)S(1)} %compare_select_fusion.8, f32[5,768,128]{2,1,0:T(8,128)S(1)} %bitcast.27), kind=kCustom, calls=%fused_computation.1.clone.clone.1 | custom fusion | flops 491520 | bytes 5898260 | tf_op jit(solution)/shard_map/while/body/eval_jaxpr/scatter-add | solution.py:66
  201.9 2.7 fusion.23
  204.6 1.9 copy.63
  206.5 6.4 %scatter_fusion = f32[768,20,128]{2,0,1:T(8,128)} fusion(f32[768,20,128]{2,0,1:T(8,128)} %get-tuple-element.294, s32[5]{0:T(128)S(1)} %compare_select_fusion.8, f32[5,768,128]{2,1,0:T(8,128)S(1)} %bitcast.27), kind=kCustom, calls=%fused_computation.1.clone.clone.1 | custom fusion | flops 491520 | bytes 5898260 | tf_op jit(solution)/shard_map/while/body/eval_jaxpr/scatter-add | solution.py:66
  216.0 2.7 fusion.23
  218.7 1.9 copy.63
  220.6 6.4 %scatter_fusion = f32[768,20,128]{2,0,1:T(8,128)} fusion(f32[768,20,128]{2,0,1:T(8,128)} %get-tuple-element.294, s32[5]{0:T(128)S(1)} %compare_select_fusion.8, f32[5,768,128]{2,1,0:T(8,128)S(1)} %bitcast.27), kind=kCustom, calls=%fused_computation.1.clone.clone.1 | custom fusion | flops 491520 | bytes 5898260 | tf_op jit(solution)/shard_map/while/body/eval_jaxpr/scatter-add | solution.py:66
  230.1 2.7 fusion.23
  232.7 1.9 copy.63
  234.6 6.4 %scatter_fusion = f32[768,20,128]{2,0,1:T(8,128)} fusion(f32[768,20,128]{2,0,1:T(8,128)} %get-tuple-element.294, s32[5]{0:T(128)S(1)} %compare_select_fusion.8, f32[5,768,128]{2,1,0:T(8,128)S(1)} %bitcast.27), kind=kCustom, calls=%fused_computation.1.clone.clone.1 | custom fusion | flops 491520 | bytes 5898260 | tf_op jit(solution)/shard_map/while/body/eval_jaxpr/scatter-add | solution.py:66
  244.1 2.7 fusion.23
  246.8 1.9 copy.63
  248.7 6.5 %scatter_fusion = f32[768,20,128]{2,0,1:T(8,128)} fusion(f32[768,20,128]{2,0,1:T(8,128)} %get-tuple-element.294, s32[5]{0:T(128)S(1)} %compare_select_fusion.8, f32[5,768,128]{2,1,0:T(8,128)S(1)} %bitcast.27), kind=kCustom, calls=%fused_computation.1.clone.clone.1 | custom fusion | flops 491520 | bytes 5898260 | tf_op jit(solution)/shard_map/while/body/eval_jaxpr/scatter-add | solution.py:66
  258.3 2.7 fusion.23
  262.8 6.4 %scatter_fusion = f32[768,20,128]{2,0,1:T(8,128)} fusion(f32[768,20,128]{2,0,1:T(8,128)} %get-tuple-element.294, s32[5]{0:T(128)S(1)} %compare_select_fusion.8, f32[5,768,128]{2,1,0:T(8,128)S(1)} %bitcast.27), kind=kCustom, calls=%fused_computation.1.clone.clone.1 | custom fusion | flops 491520 | bytes 5898260 | tf_op jit(solution)/shard_map/while/body/eval_jaxpr/scatter-add | solution.py:66
  272.3 2.7 fusion.23
  276.9 6.4 %scatter_fusion = f32[768,20,128]{2,0,1:T(8,128)} fusion(f32[768,20,128]{2,0,1:T(8,128)} %get-tuple-element.294, s32[5]{0:T(128)S(1)} %compare_select_fusion.8, f32[5,768,128]{2,1,0:T(8,128)S(1)} %bitcast.27), kind=kCustom, calls=%fused_computation.1.clone.clone.1 | custom fusion | flops 491520 | bytes 5898260 | tf_op jit(solution)/shard_map/while/body/eval_jaxpr/scatter-add | solution.py:66
  286.4 2.7 fusion.23
  291.0 6.5 %scatter_fusion = f32[768,20,128]{2,0,1:T(8,128)} fusion(f32[768,20,128]{2,0,1:T(8,128)} %get-tuple-element.294, s32[5]{0:T(128)S(1)} %compare_select_fusion.8, f32[5,768,128]{2,1,0:T(8,128)S(1)} %bitcast.27), kind=kCustom, calls=%fused_computation.1.clone.clone.1 | custom fusion | flops 491520 | bytes 5898260 | tf_op jit(solution)/shard_map/while/body/eval_jaxpr/scatter-add | solution.py:66
  300.6 2.7 fusion.23
  305.2 6.4 %scatter_fusion = f32[768,20,128]{2,0,1:T(8,128)} fusion(f32[768,20,128]{2,0,1:T(8,128)} %get-tuple-element.294, s32[5]{0:T(128)S(1)} %compare_select_fusion.8, f32[5,768,128]{2,1,0:T(8,128)S(1)} %bitcast.27), kind=kCustom, calls=%fused_computation.1.clone.clone.1 | custom fusion | flops 491520 | bytes 5898260 | tf_op jit(solution)/shard_map/while/body/eval_jaxpr/scatter-add | solution.py:66
  314.6 2.7 fusion.23
  319.2 6.5 %scatter_fusion = f32[768,20,128]{2,0,1:T(8,128)} fusion(f32[768,20,128]{2,0,1:T(8,128)} %get-tuple-element.294, s32[5]{0:T(128)S(1)} %compare_select_fusion.8, f32[5,768,128]{2,1,0:T(8,128)S(1)} %bitcast.27), kind=kCustom, calls=%fused_computation.1.clone.clone.1 | custom fusion | flops 491520 | bytes 5898260 | tf_op jit(solution)/shard_map/while/body/eval_jaxpr/scatter-add | solution.py:66
  328.7 2.7 fusion.23
  333.3 6.5 %scatter_fusion = f32[768,20,128]{2,0,1:T(8,128)} fusion(f32[768,20,128]{2,0,1:T(8,128)} %get-tuple-element.294, s32[5]{0:T(128)S(1)} %compare_select_fusion.8, f32[5,768,128]{2,1,0:T(8,128)S(1)} %bitcast.27), kind=kCustom, calls=%fused_computation.1.clone.clone.1 | custom fusion | flops 491520 | bytes 5898260 | tf_op jit(solution)/shard_map/while/body/eval_jaxpr/scatter-add | solution.py:66
  342.9 2.7 fusion.23
  347.5 6.5 %scatter_fusion = f32[768,20,128]{2,0,1:T(8,128)} fusion(f32[768,20,128]{2,0,1:T(8,128)} %get-tuple-element.294, s32[5]{0:T(128)S(1)} %compare_select_fusion.8, f32[5,768,128]{2,1,0:T(8,128)S(1)} %bitcast.27), kind=kCustom, calls=%fused_computation.1.clone.clone.1 | custom fusion | flops 491520 | bytes 5898260 | tf_op jit(solution)/shard_map/while/body/eval_jaxpr/scatter-add | solution.py:66
  357.0 2.7 fusion.23
  361.6 6.4 %scatter_fusion = f32[768,20,128]{2,0,1:T(8,128)} fusion(f32[768,20,128]{2,0,1:T(8,128)} %get-tuple-element.294, s32[5]{0:T(128)S(1)} %compare_select_fusion.8, f32[5,768,128]{2,1,0:T(8,128)S(1)} %bitcast.27), kind=kCustom, calls=%fused_computation.1.clone.clone.1 | custom fusion | flops 491520 | bytes 5898260 | tf_op jit(solution)/shard_map/while/body/eval_jaxpr/scatter-add | solution.py:66
  371.1 2.7 fusion.23
  375.7 6.5 %scatter_fusion = f32[768,20,128]{2,0,1:T(8,128)} fusion(f32[768,20,128]{2,0,1:T(8,128)} %get-tuple-element.294, s32[5]{0:T(128)S(1)} %compare_select_fusion.8, f32[5,768,128]{2,1,0:T(8,128)S(1)} %bitcast.27), kind=kCustom, calls=%fused_computation.1.clone.clone.1 | custom fusion | flops 491520 | bytes 5898260 | tf_op jit(solution)/shard_map/while/body/eval_jaxpr/scatter-add | solution.py:66
  382.2 7.2 %copy.51 = bf16[768,20,128]{0,2,1:T(8,128)(2,1)} copy(f32[768,20,128]{2,0,1:T(8,128)} %get-tuple-element.185) | data formatting | bytes 11796480 | tf_op jit(solution)/shard_map/while | solution.py:68
  389.4 6.3 %copy.52 = bf16[768,2560]{1,0:T(8,128)(2,1)} copy(bf16[768,2560]{0,1:T(8,128)(2,1)} %bitcast.29) | data formatting | bytes 7864320 | tf_op jit(solution)/shard_map/convert_element_type | solution.py:69
  (118 shorter events, 71.9 us)
Async XLA Ops:
  6.5 90.9 %all-gather.3.cloned.1.call-start = ((), (), s32[]{:S(2)}) async-start(), calls=%async_computation | async-start | bytes 3194880 | tf_op jit(solution)/shard_map/all_gather | solution.py:37
  7.3 145.4 %all-gather.5.cloned.1.call-start = ((), (), s32[]{:S(2)}) async-start(), calls=%async_computation.1 | async-start | bytes 2949120 | tf_op jit(solution)/shard_map/all_gather | solution.py:56
  10.9 4.0 copy-start
  10.9 4.0 copy-start.1
  103.5 53.1 %copy-start.2 = (s32[20]{0:T(128)S(1)}, s32[20]{0:T(128)}, u32[]{:S(2)}) copy-start(s32[20]{0:T(128)} %param.10) | copy-start | bytes 244
Sparse Core Ops, SparseCore 0:
  10.7 86.7 all-gather.2
  99.5 53.1 all-gather.4
where the time goes:
time: 405 us; the launch traced here: 402 us
  other arithmetic  157 us (39%)
  waiting for transfers between devices  132 us (33%)
  local copies, waits for them, and re-layouts  56 us (14%)
  matrix products  43.5 us (11%)
  between operations  13.5 us (3%)
    scatter-add x16, other arithmetic, one_block(): running_sum.at[:, chosen, :].add(product.reshape(occ_rows, MAXB, BLK))  103 us
    all_gather x1, waiting for transfers between devices, per_device(): gathered = lax.all_gather(amplitudes, 'vir', axis=1, tiled=True)  82.5 us
    all_gather x1, waiting for transfers between devices, per_device(): shard_piece = lax.all_gather(packed_v, 'occ', axis=0, tiled=True)  49.2 us
    dot_general x16, matrix products, one_block(): product = jnp.dot(amp_cols, block_part, preferred_element_type=jnp.float32)  43 us
    reshape x16, local copies, waits for them, and re-layouts, one_block(): product.reshape(occ_rows, MAXB, BLK)  30.2 us
    sort x17, other arithmetic, slot_order(): chosen = jnp.argsort(ranking)[:slot_bound]  27.5 us
    select_n x17, other arithmetic, slot_order(): ranking = jnp.where(matching, positions, positions + label_count)  11.5 us
    reduce_sum x16, other arithmetic, one_block(): symmetry = jnp.sum(jnp.where(block_ids == row_start // BLK, k_sym, 0))  11.1 us
  transfers between devices with their start and end apart: 2, of which 2 were waited for; matrix products, arithmetic and copies ran while one was open for 3% of the time, Pallas kernels for 0%

commit v1 on v0

--- a/solution.py
+++ b/solution.py
@@ -53,7 +53,21 @@
         preferred_element_type=jnp.float32,
     )
     packed_v = packed_v.astype(jnp.bfloat16).reshape(shard_rows, MAXB * BLK)
-    shard_piece = lax.all_gather(packed_v, "occ", axis=0, tiled=True)
+    ways, here, step = (lax.axis_size("occ"), lax.axis_index("occ"), packed_v.shape[0])
+    shape = [n * ways if d == 0 else n for d, n in enumerate(packed_v.shape)]
+    full = lax.dynamic_update_slice_in_dim(
+        jnp.zeros(shape, packed_v.dtype), packed_v, here * step, axis=0
+    )
+    going_up = going_down = packed_v
+    for far in range(1, ways // 2 + 1):
+        going_up = lax.ppermute(going_up, "occ", [(d, (d + 1) % ways) for d in range(ways)])
+        full = lax.dynamic_update_slice_in_dim(full, going_up, (here - far) % ways * step, axis=0)
+        if 2 * far < ways:
+            going_down = lax.ppermute(going_down, "occ", [(d, (d - 1) % ways) for d in range(ways)])
+            full = lax.dynamic_update_slice_in_dim(
+                full, going_down, (here + far) % ways * step, axis=0
+            )
+    shard_piece = full
     piece_blocks = shard_piece.shape[0] // BLK
 
     def one_block(block_index, running_sum):

time: 405 us -> 359 us (0.89)
  the two profiles are of different devices: /device:TPU:4 before, /device:TPU:1 now
where the time goes in v1:
time: 359 us; the launch traced here: 357 us
  other arithmetic  156 us (43%)
  local copies, waits for them, and re-layouts  64.6 us (18%)
  waiting for transfers between devices  48.8 us (14%)
  matrix products  44.3 us (12%)
  starting transfers between devices  28.3 us (8%)
  between operations  13.7 us (4%)
    scatter-add x16, other arithmetic, one_block(): running_sum.at[:, chosen, :].add(product.reshape(occ_rows, MAXB, BLK))  103 us
    dot_general x16, matrix products, one_block(): product = jnp.dot(amp_cols, block_part, preferred_element_type=jnp.float32)  43.9 us
    all_gather x1, waiting for transfers between devices, per_device(): gathered = lax.all_gather(amplitudes, 'vir', axis=1, tiled=True)  33.4 us
    reshape x16, local copies, waits for them, and re-layouts, one_block(): product.reshape(occ_rows, MAXB, BLK)  30.2 us
    sort x17, other arithmetic, slot_order(): chosen = jnp.argsort(ranking)[:slot_bound]  27.5 us
    ppermute x3, starting transfers between devices, per_device(): lax.ppermute(going_down, 'occ', [(d, (d - 1) % ways) for d in range(ways)])  17.7 us
    ppermute x4, waiting for transfers between devices, per_device(): lax.ppermute(going_up, 'occ', [(d, (d + 1) % ways) for d in range(ways)])  14.7 us
    select_n x17, other arithmetic, slot_order(): ranking = jnp.where(matching, positions, positions + label_count)  11.5 us
  transfers between devices with their start and end apart: 8, of which 5 were waited for; matrix products, arithmetic and copies ran while one was open for 5% of the time, Pallas kernels for 0%

profile of v1, /device:TPU:1, one launch (start us, length us, event | category | flops | bytes accessed | tf_op | source)
XLA Modules:
  0.0 356.6 jit_solution(6170751198216672941)
XLA Ops:
  10.9 2.5 reshape.82
  16.6 4.9 %collective-permute-start = (bf16[256,640]{0,1:T(8,128)(2,1)S(1)}, bf16[256,640]{0,1:T(8,128)(2,1)S(1)}, u32[]{:S(2)}, u32[]{:S(2)}) collective-permute-start(bf16[256,640]{0,1:T(8,128)(2,1)S(1)} %copy.83), channel_id=1, source_target_pairs={{0,64},{64,128},{128,192},{192,256},{256,320},{320,384},{384,448},... | collective-permute-start | bytes 983048 | tf_op jit(solution)/shard_map/ppermute | solution.py:63
  21.5 8.6 %collective-permute-start.1 = (bf16[256,640]{0,1:T(8,128)(2,1)S(1)}, bf16[256,640]{0,1:T(8,128)(2,1)S(1)}, u32[]{:S(2)}, u32[]{:S(2)}) collective-permute-start(bf16[256,640]{0,1:T(8,128)(2,1)S(1)} %copy.83), channel_id=1, source_target_pairs={{0,448},{64,0},{128,64},{192,128},{256,192},{320,256},{384,320},{4... | collective-permute-start | bytes 983048 | tf_op jit(solution)/shard_map/ppermute | solution.py:66
  30.0 5.5 %collective-permute-done = bf16[256,640]{0,1:T(8,128)(2,1)S(1)} collective-permute-done((bf16[256,640]{0,1:T(8,128)(2,1)S(1)}, bf16[256,640]{0,1:T(8,128)(2,1)S(1)}, u32[]{:S(2)}, u32[]{:S(2)}) %collective-permute-start) | collective-permute-done | bytes 327712 | tf_op jit(solution)/shard_map/ppermute | solution.py:63
  35.5 1.9 collective-permute-start.2
  37.6 4.6 %collective-permute-start.3 = (bf16[256,640]{0,1:T(8,128)(2,1)S(1)}, bf16[256,640]{0,1:T(8,128)(2,1)S(1)}, u32[]{:S(2)}, u32[]{:S(2)}) collective-permute-start(bf16[256,640]{0,1:T(8,128)(2,1)S(1)} %collective-permute-done.1), channel_id=1, source_target_pairs={{0,448},{64,0},{128,64},{192,128},{256,192},{320,256},{384,320},{4... | collective-permute-start | bytes 983048 | tf_op jit(solution)/shard_map/ppermute | solution.py:66
  42.7 3.9 %collective-permute-done.2 = bf16[256,640]{0,1:T(8,128)(2,1)S(1)} collective-permute-done((bf16[256,640]{0,1:T(8,128)(2,1)S(1)}, bf16[256,640]{0,1:T(8,128)(2,1)S(1)}, u32[]{:S(2)}, u32[]{:S(2)}) %collective-permute-start.2) | collective-permute-done | bytes 327712 | tf_op jit(solution)/shard_map/ppermute | solution.py:63
  49.3 4.6 %collective-permute-start.5 = (bf16[256,640]{0,1:T(8,128)(2,1)S(1)}, bf16[256,640]{0,1:T(8,128)(2,1)S(1)}, u32[]{:S(2)}, u32[]{:S(2)}) collective-permute-start(bf16[256,640]{0,1:T(8,128)(2,1)S(1)} %collective-permute-done.3), channel_id=1, source_target_pairs={{0,448},{64,0},{128,64},{192,128},{256,192},{320,256},{384,320},{4... | collective-permute-start | bytes 983048 | tf_op jit(solution)/shard_map/ppermute | solution.py:66
  61.4 4.4 %collective-permute-done.6 = bf16[256,640]{0,1:T(8,128)(2,1)S(1)} collective-permute-done((bf16[256,640]{0,1:T(8,128)(2,1)S(1)}, bf16[256,640]{0,1:T(8,128)(2,1)S(1)}, u32[]{:S(2)}, u32[]{:S(2)}) %collective-permute-start.6) | collective-permute-done | bytes 327712 | tf_op jit(solution)/shard_map/ppermute | solution.py:63
  66.7 33.4 %all-gather.2.cloned.1.call-done = bf16[768,2048]{0,1:T(8,128)(2,1)} async-done(((bf16[768,32]{0,1:T(8,128)(2,1)}), bf16[768,2048]{0,1:T(8,128)(2,1)}) %all-gather.2.cloned.1.call-update) | async-done | bytes 3145744 | tf_op jit(solution)/shard_map/all_gather | solution.py:37
  100.2 3.2 copy.64
  103.8 2.4 bitcast_multiply_fusion
  106.2 3.9 %broadcast_in_dim.65 = f32[768,20,128]{2,0,1:T(8,128)} broadcast(f32[]{:T(128)} %constant.138.clone.1), dimensions={} | broadcast | bytes 7864324 | tf_op jit(solution)/shard_map/broadcast_in_dim | solution.py:47
  110.1 226.1 %while.16 = (s32[]{:T(128)}, f32[768,20,128]{2,0,1:T(8,128)}, s32[16]{0:T(128)S(1)}, s32[20]{0:T(128)S(1)}, bf16[768,2048]{1,0:T(8,128)(2,1)}, /*index=5*/bf16[2...) while((s32[]{:T(128)}, f32[768,20,128]{2,0,1:T(8,128)}, ...), condition=%wide.region_6.7_spmd.clone, body=%wide.region_2.6_spmd.clone.sunk | while | flops 126320880 | bytes 12158960 | solution.py:82
  113.2 2.7 fusion.23
  117.8 6.5 %scatter_fusion = f32[768,20,128]{2,0,1:T(8,128)} fusion(f32[768,20,128]{2,0,1:T(8,128)} %get-tuple-element.278, s32[5]{0:T(128)S(1)} %compare_select_fusion.8, f32[5,768,128]{2,1,0:T(8,128)S(1)} %bitcast.27), kind=kCustom, calls=%fused_computation.1.clone.clone.1 | custom fusion | flops 491520 | bytes 5898260 | tf_op jit(solution)/shard_map/while/body/eval_jaxpr/scatter-add | solution.py:80
  127.4 2.7 fusion.23
  132.0 6.4 %scatter_fusion = f32[768,20,128]{2,0,1:T(8,128)} fusion(f32[768,20,128]{2,0,1:T(8,128)} %get-tuple-element.278, s32[5]{0:T(128)S(1)} %compare_select_fusion.8, f32[5,768,128]{2,1,0:T(8,128)S(1)} %bitcast.27), kind=kCustom, calls=%fused_computation.1.clone.clone.1 | custom fusion | flops 491520 | bytes 5898260 | tf_op jit(solution)/shard_map/while/body/eval_jaxpr/scatter-add | solution.py:80
  141.5 2.7 fusion.23
  146.1 6.5 %scatter_fusion = f32[768,20,128]{2,0,1:T(8,128)} fusion(f32[768,20,128]{2,0,1:T(8,128)} %get-tuple-element.278, s32[5]{0:T(128)S(1)} %compare_select_fusion.8, f32[5,768,128]{2,1,0:T(8,128)S(1)} %bitcast.27), kind=kCustom, calls=%fused_computation.1.clone.clone.1 | custom fusion | flops 491520 | bytes 5898260 | tf_op jit(solution)/shard_map/while/body/eval_jaxpr/scatter-add | solution.py:80
  155.7 2.7 fusion.23
  160.3 6.4 %scatter_fusion = f32[768,20,128]{2,0,1:T(8,128)} fusion(f32[768,20,128]{2,0,1:T(8,128)} %get-tuple-element.278, s32[5]{0:T(128)S(1)} %compare_select_fusion.8, f32[5,768,128]{2,1,0:T(8,128)S(1)} %bitcast.27), kind=kCustom, calls=%fused_computation.1.clone.clone.1 | custom fusion | flops 491520 | bytes 5898260 | tf_op jit(solution)/shard_map/while/body/eval_jaxpr/scatter-add | solution.py:80
  169.8 2.7 fusion.23
  174.4 6.4 %scatter_fusion = f32[768,20,128]{2,0,1:T(8,128)} fusion(f32[768,20,128]{2,0,1:T(8,128)} %get-tuple-element.278, s32[5]{0:T(128)S(1)} %compare_select_fusion.8, f32[5,768,128]{2,1,0:T(8,128)S(1)} %bitcast.27), kind=kCustom, calls=%fused_computation.1.clone.clone.1 | custom fusion | flops 491520 | bytes 5898260 | tf_op jit(solution)/shard_map/while/body/eval_jaxpr/scatter-add | solution.py:80
  183.9 2.7 fusion.23
  188.6 6.4 %scatter_fusion = f32[768,20,128]{2,0,1:T(8,128)} fusion(f32[768,20,128]{2,0,1:T(8,128)} %get-tuple-element.278, s32[5]{0:T(128)S(1)} %compare_select_fusion.8, f32[5,768,128]{2,1,0:T(8,128)S(1)} %bitcast.27), kind=kCustom, calls=%fused_computation.1.clone.clone.1 | custom fusion | flops 491520 | bytes 5898260 | tf_op jit(solution)/shard_map/while/body/eval_jaxpr/scatter-add | solution.py:80
  198.1 2.7 fusion.23
  202.7 6.4 %scatter_fusion = f32[768,20,128]{2,0,1:T(8,128)} fusion(f32[768,20,128]{2,0,1:T(8,128)} %get-tuple-element.278, s32[5]{0:T(128)S(1)} %compare_select_fusion.8, f32[5,768,128]{2,1,0:T(8,128)S(1)} %bitcast.27), kind=kCustom, calls=%fused_computation.1.clone.clone.1 | custom fusion | flops 491520 | bytes 5898260 | tf_op jit(solution)/shard_map/while/body/eval_jaxpr/scatter-add | solution.py:80
  212.2 2.7 fusion.23
  216.8 6.4 %scatter_fusion = f32[768,20,128]{2,0,1:T(8,128)} fusion(f32[768,20,128]{2,0,1:T(8,128)} %get-tuple-element.278, s32[5]{0:T(128)S(1)} %compare_select_fusion.8, f32[5,768,128]{2,1,0:T(8,128)S(1)} %bitcast.27), kind=kCustom, calls=%fused_computation.1.clone.clone.1 | custom fusion | flops 491520 | bytes 5898260 | tf_op jit(solution)/shard_map/while/body/eval_jaxpr/scatter-add | solution.py:80
  226.3 2.7 fusion.23
  230.9 6.4 %scatter_fusion = f32[768,20,128]{2,0,1:T(8,128)} fusion(f32[768,20,128]{2,0,1:T(8,128)} %get-tuple-element.278, s32[5]{0:T(128)S(1)} %compare_select_fusion.8, f32[5,768,128]{2,1,0:T(8,128)S(1)} %bitcast.27), kind=kCustom, calls=%fused_computation.1.clone.clone.1 | custom fusion | flops 491520 | bytes 5898260 | tf_op jit(solution)/shard_map/while/body/eval_jaxpr/scatter-add | solution.py:80
  240.4 2.7 fusion.23
  245.1 6.4 %scatter_fusion = f32[768,20,128]{2,0,1:T(8,128)} fusion(f32[768,20,128]{2,0,1:T(8,128)} %get-tuple-element.278, s32[5]{0:T(128)S(1)} %compare_select_fusion.8, f32[5,768,128]{2,1,0:T(8,128)S(1)} %bitcast.27), kind=kCustom, calls=%fused_computation.1.clone.clone.1 | custom fusion | flops 491520 | bytes 5898260 | tf_op jit(solution)/shard_map/while/body/eval_jaxpr/scatter-add | solution.py:80
  254.5 2.7 fusion.23
  259.2 6.4 %scatter_fusion = f32[768,20,128]{2,0,1:T(8,128)} fusion(f32[768,20,128]{2,0,1:T(8,128)} %get-tuple-element.278, s32[5]{0:T(128)S(1)} %compare_select_fusion.8, f32[5,768,128]{2,1,0:T(8,128)S(1)} %bitcast.27), kind=kCustom, calls=%fused_computation.1.clone.clone.1 | custom fusion | flops 491520 | bytes 5898260 | tf_op jit(solution)/shard_map/while/body/eval_jaxpr/scatter-add | solution.py:80
  268.7 2.7 fusion.23
  273.3 6.4 %scatter_fusion = f32[768,20,128]{2,0,1:T(8,128)} fusion(f32[768,20,128]{2,0,1:T(8,128)} %get-tuple-element.278, s32[5]{0:T(128)S(1)} %compare_select_fusion.8, f32[5,768,128]{2,1,0:T(8,128)S(1)} %bitcast.27), kind=kCustom, calls=%fused_computation.1.clone.clone.1 | custom fusion | flops 491520 | bytes 5898260 | tf_op jit(solution)/shard_map/while/body/eval_jaxpr/scatter-add | solution.py:80
  282.8 2.7 fusion.23
  287.4 6.4 %scatter_fusion = f32[768,20,128]{2,0,1:T(8,128)} fusion(f32[768,20,128]{2,0,1:T(8,128)} %get-tuple-element.278, s32[5]{0:T(128)S(1)} %compare_select_fusion.8, f32[5,768,128]{2,1,0:T(8,128)S(1)} %bitcast.27), kind=kCustom, calls=%fused_computation.1.clone.clone.1 | custom fusion | flops 491520 | bytes 5898260 | tf_op jit(solution)/shard_map/while/body/eval_jaxpr/scatter-add | solution.py:80
  296.9 2.7 fusion.23
  301.5 6.5 %scatter_fusion = f32[768,20,128]{2,0,1:T(8,128)} fusion(f32[768,20,128]{2,0,1:T(8,128)} %get-tuple-element.278, s32[5]{0:T(128)S(1)} %compare_select_fusion.8, f32[5,768,128]{2,1,0:T(8,128)S(1)} %bitcast.27), kind=kCustom, calls=%fused_computation.1.clone.clone.1 | custom fusion | flops 491520 | bytes 5898260 | tf_op jit(solution)/shard_map/while/body/eval_jaxpr/scatter-add | solution.py:80
  311.1 2.7 fusion.23
  315.7 6.4 %scatter_fusion = f32[768,20,128]{2,0,1:T(8,128)} fusion(f32[768,20,128]{2,0,1:T(8,128)} %get-tuple-element.278, s32[5]{0:T(128)S(1)} %compare_select_fusion.8, f32[5,768,128]{2,1,0:T(8,128)S(1)} %bitcast.27), kind=kCustom, calls=%fused_computation.1.clone.clone.1 | custom fusion | flops 491520 | bytes 5898260 | tf_op jit(solution)/shard_map/while/body/eval_jaxpr/scatter-add | solution.py:80
  325.2 2.7 fusion.23
  329.8 6.4 %scatter_fusion = f32[768,20,128]{2,0,1:T(8,128)} fusion(f32[768,20,128]{2,0,1:T(8,128)} %get-tuple-element.278, s32[5]{0:T(128)S(1)} %compare_select_fusion.8, f32[5,768,128]{2,1,0:T(8,128)S(1)} %bitcast.27), kind=kCustom, calls=%fused_computation.1.clone.clone.1 | custom fusion | flops 491520 | bytes 5898260 | tf_op jit(solution)/shard_map/while/body/eval_jaxpr/scatter-add | solution.py:80
  336.3 7.2 %copy.79 = bf16[768,20,128]{0,2,1:T(8,128)(2,1)} copy(f32[768,20,128]{2,0,1:T(8,128)} %get-tuple-element.185) | data formatting | bytes 11796480 | tf_op jit(solution)/shard_map/while | solution.py:82
  343.4 6.3 %copy.80 = bf16[768,2560]{1,0:T(8,128)(2,1)} copy(bf16[768,2560]{0,1:T(8,128)(2,1)} %bitcast.29) | data formatting | bytes 7864320 | tf_op jit(solution)/shard_map/convert_element_type | solution.py:83
  (144 shorter events, 98.4 us)
Async XLA Ops:
  6.5 93.6 %all-gather.2.cloned.1.call-start = ((), (), s32[]{:S(2)}) async-start(), calls=%async_computation | async-start | bytes 3194880 | tf_op jit(solution)/shard_map/all_gather | solution.py:37
  13.8 28.3 %copy-start = (s32[6]{0:T(128)S(1)}, s32[6]{0:T(128)}, u32[]{:S(2)}) copy-start(s32[6]{0:T(128)} %param.9) | copy-start | bytes 76
  13.9 28.3 %copy-start.1 = (s32[16]{0:T(128)S(1)}, s32[16]{0:T(128)}, u32[]{:S(2)}) copy-start(s32[16]{0:T(128)} %param.11) | copy-start | bytes 196
  16.6 18.9 %collective-permute-start = (bf16[256,640]{0,1:T(8,128)(2,1)S(1)}, bf16[256,640]{0,1:T(8,128)(2,1)S(1)}, u32[]{:S(2)}, u32[]{:S(2)}) collective-permute-start(bf16[256,640]{0,1:T(8,128)(2,1)S(1)} %copy.83), channel_id=1, source_target_pairs={{0,64},{64,128},{128,192},{192,256},{256,320},{320,384},{384,448},... | collective-permute-start | bytes 983048 | tf_op jit(solution)/shard_map/ppermute | solution.py:63
  21.5 16.1 %collective-permute-start.1 = (bf16[256,640]{0,1:T(8,128)(2,1)S(1)}, bf16[256,640]{0,1:T(8,128)(2,1)S(1)}, u32[]{:S(2)}, u32[]{:S(2)}) collective-permute-start(bf16[256,640]{0,1:T(8,128)(2,1)S(1)} %copy.83), channel_id=1, source_target_pairs={{0,448},{64,0},{128,64},{192,128},{256,192},{320,256},{384,320},{4... | collective-permute-start | bytes 983048 | tf_op jit(solution)/shard_map/ppermute | solution.py:66
  35.5 11.1 %collective-permute-start.2 = (bf16[256,640]{0,1:T(8,128)(2,1)S(1)}, bf16[256,640]{0,1:T(8,128)(2,1)S(1)}, u32[]{:S(2)}, u32[]{:S(2)}) collective-permute-start(bf16[256,640]{0,1:T(8,128)(2,1)S(1)} %collective-permute-done), channel_id=1, source_target_pairs={{0,64},{64,128},{128,192},{192,256},{256,320},{320,384},{384,448},... | collective-permute-start | bytes 983048 | tf_op jit(solution)/shard_map/ppermute | solution.py:63
  37.6 11.7 %collective-permute-start.3 = (bf16[256,640]{0,1:T(8,128)(2,1)S(1)}, bf16[256,640]{0,1:T(8,128)(2,1)S(1)}, u32[]{:S(2)}, u32[]{:S(2)}) collective-permute-start(bf16[256,640]{0,1:T(8,128)(2,1)S(1)} %collective-permute-done.1), channel_id=1, source_target_pairs={{0,448},{64,0},{128,64},{192,128},{256,192},{320,256},{384,320},{4... | collective-permute-start | bytes 983048 | tf_op jit(solution)/shard_map/ppermute | solution.py:66
  46.6 10.1 %collective-permute-start.4 = (bf16[256,640]{0,1:T(8,128)(2,1)S(1)}, bf16[256,640]{0,1:T(8,128)(2,1)S(1)}, u32[]{:S(2)}, u32[]{:S(2)}) collective-permute-start(bf16[256,640]{0,1:T(8,128)(2,1)S(1)} %collective-permute-done.2), channel_id=1, source_target_pairs={{0,64},{64,128},{128,192},{192,256},{256,320},{320,384},{384,448},... | collective-permute-start | bytes 983048 | tf_op jit(solution)/shard_map/ppermute | solution.py:63
  49.3 10.4 %collective-permute-start.5 = (bf16[256,640]{0,1:T(8,128)(2,1)S(1)}, bf16[256,640]{0,1:T(8,128)(2,1)S(1)}, u32[]{:S(2)}, u32[]{:S(2)}) collective-permute-start(bf16[256,640]{0,1:T(8,128)(2,1)S(1)} %collective-permute-done.3), channel_id=1, source_target_pairs={{0,448},{64,0},{128,64},{192,128},{256,192},{320,256},{384,320},{4... | collective-permute-start | bytes 983048 | tf_op jit(solution)/shard_map/ppermute | solution.py:66
  56.7 9.0 %collective-permute-start.6 = (bf16[256,640]{0,1:T(8,128)(2,1)S(1)}, bf16[256,640]{0,1:T(8,128)(2,1)S(1)}, u32[]{:S(2)}, u32[]{:S(2)}) collective-permute-start(bf16[256,640]{0,1:T(8,128)(2,1)S(1)} %collective-permute-done.4), channel_id=1, source_target_pairs={{0,64},{64,128},{128,192},{192,256},{256,320},{320,384},{384,448},... | collective-permute-start | bytes 983048 | tf_op jit(solution)/shard_map/ppermute | solution.py:63
  106.2 3.9 %copy-start.2 = (s32[20]{0:T(128)S(1)}, s32[20]{0:T(128)}, u32[]{:S(2)}) copy-start(s32[20]{0:T(128)} %param.10) | copy-start | bytes 244
Sparse Core Ops, SparseCore 0:
  10.7 89.4 all-gather.1
